TPU v7x, 32 devices: a whole 2x2x4 slice. The times are simulated.
32 devices in a mesh: inv: 2 (over y), test: 2 (over core), tx: 4 (over z), ty: 2 (over x).
Axes of the slice: x: 2, y: 2, z: 4, core: 2. Of those that a mesh axis runs over, the one named last changes fastest.
Arguments:
- log_cond: float32 [2560, 512], P(('inv', 'tx'), 'ty'), parts along dimension 0, may hold values from -3.5 to -1.7
- log_shape: float32 [2560, 512], P(('inv', 'tx'), 'ty'), parts along dimension 0, may hold values from -2.8 to -1.6
- zone_ids: int32 [2560, 512], P(('inv', 'tx'), 'ty'), parts along dimension 0, may hold values from 0 to 7
- storage: float32 [4, 8], P('inv'), parts along dimension 0, may hold values from 0.9 to 1.2
- pump_x: int32 [4, 1], P(('inv', 'test')), parts along dimension 0, may hold values from 0 to 1279
- pump_y: int32 [4, 1], P(('inv', 'test')), parts along dimension 0, may hold values from 0 to 511
- pump_rates: float32 [4, 3, 1], P(('inv', 'test')), parts along dimension 0, may hold values from -4 to -1
- obs_x: int32 [128], P('inv'), parts along dimension 0, may hold values from 0 to 1279
- obs_y: int32 [128], P('inv'), parts along dimension 0, may hold values from 0 to 511
- observed: float32 [4, 3, 64], P(('inv', 'test')), parts along dimension 0, may hold values from -6 to 6
- frac_start: float32 [4, 1280, 512], P(('inv', 'test'), 'tx', 'ty'), parts along dimension 0, may hold values from -6 to 6
- matrix_start: float32 [4, 1280, 512], P(('inv', 'test'), 'tx', 'ty'), parts along dimension 0, may hold values from -6 to 6
- frac_end: float32 [4, 1280, 512], P(('inv', 'test'), 'tx', 'ty'), parts along dimension 0, may hold values from -6 to 6
- matrix_end: float32 [4, 1280, 512], P(('inv', 'test'), 'tx', 'ty'), parts along dimension 0, may hold values from -6 to 6
Outputs:
- cond_direction: float32 [2560, 512], P(('inv', 'tx'), 'ty'), parts along dimension 0
- shape_direction: float32 [2560, 512], P(('inv', 'tx'), 'ty'), parts along dimension 0
- frac_adjoint: float32 [4, 1280, 512], P(('inv', 'test'), 'tx', 'ty'), parts along dimension 0
- matrix_adjoint: float32 [4, 1280, 512], P(('inv', 'test'), 'tx', 'ty'), parts along dimension 0
There are 2 independent parts, one for each index of `inv`. A program takes and returns all parts, laid end to end along the dimension named above; each array names one. Nothing has to cross between parts.
All inputs are finite; a program needn't handle non-finite values.
Results may differ from a plain program's by a relative error of at most 0.0001.
Values sent between devices are 32-bit elements; how exact they have to be, the bound alone decides.
No kernel may reach another device: no remote copies, remote signals or barrier semaphores. Data moves between devices by JAX's collectives and lax.ppermute only.
A program may use at most 64 MiB of HBM per device.

v0:
```python
import jax
import jax.numpy as jnp
from jax import lax
from jax.sharding import PartitionSpec as P

SMOOTH = 2
blend_rate = 0.2


def padded_2(cells, sides, width):
    for axis, dim in sides:
        count = lax.axis_size(axis)
        ends = count - 1
        head = lax.slice_in_dim(cells, 0, width, axis=dim)
        tail = lax.slice_in_dim(cells, cells.shape[dim] - width, cells.shape[dim], axis=dim)
        cells = jnp.concatenate(
            [
                lax.ppermute(tail, axis, [(i, (i + 1) % count) for i in range(ends)]),
                cells,
                lax.ppermute(head, axis, [((i + 1) % count, i) for i in range(ends)]),
            ],
            axis=dim,
        )
    return cells


def neighbours(padded):
    return (
        padded[..., :-2, 1:-1],
        padded[..., 2:, 1:-1],
        padded[..., 1:-1, :-2],
        padded[..., 1:-1, 2:],
    )


def flow_sum(padded, conductances):
    centre = padded[..., 1:-1, 1:-1]
    summed = jnp.zeros_like(centre)
    for conductance, beside in zip(conductances, neighbours(padded)):
        summed = summed + conductance * (beside - centre)
    return summed


def zero_border(field):
    return jnp.pad(field, [(0, 0)] * (field.ndim - 2) + [(1, 1), (1, 1)])


def local_spots(coord_x, coord_y, tile_rows, tile_cols, margin):
    local_x = coord_x - lax.axis_index("tx") * tile_rows + margin
    local_y = coord_y - lax.axis_index("ty") * tile_cols + margin
    extent_x = tile_rows + 2 * margin
    extent_y = tile_cols + 2 * margin
    inside = (local_x >= 0) & (local_x < extent_x) & (local_y >= 0) & (local_y < extent_y)
    return (jnp.clip(local_x, 0, extent_x - 1), jnp.clip(local_y, 0, extent_y - 1), inside)


def smooth(grad_field):
    for sweep_index in range(SMOOTH):
        padded = padded_2(grad_field, (("tx", 1), ("ty", 2)), 1)
        nearby = neighbours(padded)
        grad_field = grad_field + blend_rate * (
            nearby[0] + nearby[1] + nearby[2] + nearby[3] - 4.0 * grad_field
        )
    return grad_field


def margin_window(
    cond,
    shape_factor,
    store_frac,
    store_matrix,
    pump_x,
    pump_y,
    pump_rates,
    obs_x,
    obs_y,
    observed,
    frac_start,
    matrix_start,
    frac_end,
    matrix_end,
):
    tile_rows, tile_cols = cond.shape
    test_count = frac_start.shape[0]
    step_count = pump_rates.shape[1]
    margin = 2 * step_count
    packed = jnp.concatenate(
        [
            cond[None],
            shape_factor[None],
            store_frac[None],
            store_matrix[None],
            frac_start,
            matrix_start,
            frac_end,
            matrix_end,
        ],
        0,
    )
    widened = padded_2(packed, (("tx", 1), ("ty", 2)), margin)
    place_x = lax.axis_index("tx") * tile_rows - margin + jnp.arange(tile_rows + 2 * margin)
    place_y = lax.axis_index("ty") * tile_cols - margin + jnp.arange(tile_cols + 2 * margin)
    within = ((place_x >= 0) & (place_x < tile_rows * lax.axis_size("tx")))[:, None] & (
        (place_y >= 0) & (place_y < tile_cols * lax.axis_size("ty"))
    )[None, :]
    cond_wide = widened[0]
    shape_wide = widened[1]
    sfrac_wide = jnp.where(within, widened[2], 1.0)
    smatrix_wide = jnp.where(within, widened[3], 1.0)
    fracture = widened[4 : 4 + test_count]
    matrix = widened[4 + test_count : 4 + 2 * test_count]
    end_frac = widened[4 + 2 * test_count : 4 + 3 * test_count]
    end_matrix = widened[4 + 3 * test_count : 4 + 4 * test_count]
    cond_nearby = neighbours(zero_border(cond_wide))
    conductances = []
    slopes = []
    for beside in cond_nearby:
        total = cond_wide + beside
        safe_total = jnp.where(total > 0.0, total, 1.0)
        conductances.append(2.0 * cond_wide * beside / safe_total)
        slopes.append(2.0 * beside * beside / (safe_total * safe_total))
    spot_x, spot_y, spot_in = local_spots(pump_x, pump_y, tile_rows, tile_cols, margin)
    test_rows = jnp.arange(test_count)[:, None]
    obs_lx, obs_ly, obs_in = local_spots(obs_x, obs_y, tile_rows, tile_cols, margin)
    stored = []
    mismatches = []
    for step_index in range(step_count):
        stored.append((fracture, matrix))
        transfer = shape_wide * (fracture - matrix)
        source = (
            jnp.zeros_like(fracture)
            .at[test_rows, spot_x, spot_y]
            .add(jnp.where(spot_in, pump_rates[:, step_index], 0.0))
        )
        fracture_next = (
            fracture
            + (flow_sum(zero_border(fracture), conductances) - transfer + source) / sfrac_wide
        )
        matrix = matrix + transfer / smatrix_wide
        fracture = fracture_next
        mismatches.append(
            jnp.where(obs_in[None], fracture[:, obs_lx, obs_ly] - observed[:, step_index], 0.0)
        )

    def inject(adjoint_field, mismatch):
        return adjoint_field.at[:, obs_lx, obs_ly].add(mismatch)

    def interior(field):
        return field[..., margin : margin + tile_rows, margin : margin + tile_cols]

    fracture_adj = inject(end_frac, mismatches[step_count - 1])
    matrix_adj = end_matrix
    grad_cond = jnp.zeros((tile_rows, tile_cols), jnp.float32)
    grad_shape = jnp.zeros((tile_rows, tile_cols), jnp.float32)
    for step_index in reversed(range(step_count)):
        fracture, matrix = stored[step_index]
        scaled = fracture_adj / sfrac_wide
        matrix_scaled = matrix_adj / smatrix_wide
        scaled_pad = zero_border(scaled)
        spread = flow_sum(scaled_pad, conductances)
        face_term = jnp.zeros_like(fracture)
        for slope, head_beside, adjoint_beside in zip(
            slopes, neighbours(zero_border(fracture)), neighbours(scaled_pad)
        ):
            face_term = face_term + slope * (head_beside - fracture) * (scaled - adjoint_beside)
        grad_cond = grad_cond + interior(cond_wide * jnp.sum(face_term, axis=0))
        swap_rate = shape_wide * (matrix_scaled - scaled)
        grad_shape = grad_shape + interior(jnp.sum(swap_rate * (fracture - matrix), axis=0))
        fracture_adj = fracture_adj + spread + swap_rate
        matrix_adj = matrix_adj - swap_rate
        if step_index > 0:
            fracture_adj = inject(fracture_adj, mismatches[step_index - 1])
    return (grad_cond, grad_shape, interior(fracture_adj), interior(matrix_adj))


def on_device(
    log_cond,
    log_shape,
    zone_ids,
    storage,
    pump_x,
    pump_y,
    pump_rates,
    obs_x,
    obs_y,
    observed,
    frac_start,
    matrix_start,
    frac_end,
    matrix_end,
):
    cond = jnp.exp(log_cond)
    shape_factor = jnp.exp(log_shape)
    store_frac = jnp.zeros_like(cond)
    store_matrix = jnp.zeros_like(cond)
    for zone_index in range(storage.shape[1]):
        chosen = zone_ids == zone_index
        store_frac = jnp.where(chosen, storage[0, zone_index], store_frac)
        store_matrix = jnp.where(chosen, storage[1, zone_index], store_matrix)
    grad_cond, grad_shape, fracture_adj, matrix_adj = margin_window(
        cond,
        shape_factor,
        store_frac,
        store_matrix,
        pump_x,
        pump_y,
        pump_rates,
        obs_x,
        obs_y,
        observed,
        frac_start,
        matrix_start,
        frac_end,
        matrix_end,
    )
    stacked = jnp.stack([grad_cond, grad_shape], 0)
    summed = lax.psum(stacked, "test")
    smoothed = smooth(summed)
    return (smoothed[0], smoothed[1], fracture_adj, matrix_adj)


def solution(mesh):
    placed = (
        P(("inv", "tx"), "ty"),
        P(("inv", "tx"), "ty"),
        P(("inv", "tx"), "ty"),
        P("inv", None),
        P(("inv", "test"), None),
        P(("inv", "test"), None),
        P(("inv", "test"), None, None),
        P("inv"),
        P("inv"),
        P(("inv", "test"), None, None),
        P(("inv", "test"), "tx", "ty"),
        P(("inv", "test"), "tx", "ty"),
        P(("inv", "test"), "tx", "ty"),
        P(("inv", "test"), "tx", "ty"),
    )
    return jax.shard_map(
        on_device,
        mesh=mesh,
        in_specs=placed,
        out_specs=(
            P(("inv", "tx"), "ty"),
            P(("inv", "tx"), "ty"),
            P(("inv", "test"), "tx", "ty"),
            P(("inv", "test"), "tx", "ty"),
        ),
        check_vma=False,
    )
```

profile of v0, /device:TPU:0, one launch (start us, length us, event | category | flops | bytes accessed | tf_op | source)
XLA Modules:
  0.0 218.5 jit_solution(2237124378234032437)
XLA Ops:
  7.2 2.0 fusion.52
  9.2 1.9 copy.72
  11.1 1.9 copy.73
  13.0 1.9 copy.74
  14.9 1.9 copy.82
  16.8 1.9 copy.83
  22.0 6.5 %bitcast_dynamic-update-slice_fusion.1 = (f32[8,320,256]{1,2,0:T(8,128)S(1)}, pred[320,256]{0,1:T(8,128)(4,1)S(1)}, pred[320,256]{0,1:T(8,128)(4,1)S(1)}, pred[3...) fusion(f32[8,320,256]{1,2,0:T(8,128)S(1)} %bitcast_dynamic-upda, ...), kind=kLoop, calls=%fused_computation.121 | loop fusion | flops 1310720 | bytes 1507360
  28.5 5.3 %bitcast_dynamic-update-slice_fusion = f32[8,320,256]{1,2,0:T(8,128)S(1)} fusion(f32[8,320,256]{1,2,0:T(8,128)S(1)} %get-tuple-element.72, pred[320,256]{0,1:T(8,128)(4,1)S(1)} %get-tuple-element.80, pred[320,256]{0,1:T(8,128)(4,1)S(1)} %get-tuple-element.79, pred[320,256]{0,1:T(8,128)(4,1)S(1)} %get-tuple-element.78, ...), kind=kLoop, calls=%fused_computation.120 | loop fusion | flops 655360 | bytes 1179680
  34.1 1.9 fusion.49
  36.0 1.5 copy.87
  38.9 1.6 copy.86
  40.4 5.6 %collective-permute-start = (f32[8,6,256]{2,0,1:T(8,128)S(1)}, f32[8,6,256]{2,0,1:T(8,128)S(1)}, u32[]{:S(2)}, u32[]{:S(2)}) collective-permute-start(f32[8,6,256]{2,0,1:T(8,128)S(1)} %copy.86), channel_id=1, source_target_pairs={{0,2},{2,4},{4,6},{1,3},{3,5},{5,7},{8,10},{10,12},{12,14},{9,11},... | collective-permute-start | bytes 147464 | tf_op jit(solution)/shard_map/ppermute | solution.py:18
  52.8 1.4 copy.88
  56.6 3.8 %collective-permute-start.2 = (f32[8,332,6]{1,2,0:T(8,128)S(1)}, f32[8,332,6]{1,2,0:T(8,128)S(1)}, u32[]{:S(2)}, u32[]{:S(2)}) collective-permute-start(f32[8,332,6]{1,2,0:T(8,128)S(1)} %get-tuple-element.81), channel_id=1, source_target_pairs={{0,1},{2,3},{4,5},{6,7},{8,9},{10,11},{12,13},{14,15},{16,17},{18,... | collective-permute-start | bytes 191240 | tf_op jit(solution)/shard_map/ppermute | solution.py:18
  62.6 4.3 %collective-permute-done.3 = f32[8,332,6]{1,2,0:T(8,128)S(1)} collective-permute-done((f32[8,332,6]{1,2,0:T(8,128)S(1)}, f32[8,332,6]{1,2,0:T(8,128)S(1)}, u32[]{:S(2)}, u32[]{:S(2)}) %collective-permute-start.3) | collective-permute-done | bytes 63776 | tf_op jit(solution)/shard_map/ppermute | solution.py:20
  66.9 3.2 %pad_maximum_fusion = f32[8,332,268]{1,2,0:T(8,128)S(1)} fusion(f32[8,332,6]{1,2,0:T(8,128)S(1)} %collective-permute-done.3, f32[8,6,256]{1,2,0:T(8,128)S(1)} %copy-done.17, f32[8,320,256]{1,2,0:T(8,128)} %copy-done, f32[8,6,256]{1,2,0:T(8,128)S(1)} %copy-done.16, f32[8,332,6]{1,2,0:T(8,128)S(1)} %collective-permute-done.2), kind=kLoop, calls=%fused_computation.6 | loop fusion | flops 2847232 | bytes 5694464 | tf_op jit(solution)/shard_map/concatenate | solution.py:16
  71.0 1.9 add_subtract_fusion.2
  75.0 1.4 add.283
  78.3 2.8 %add_subtract_fusion.1 = (f32[1,332,268]{1,2,0:T(8,128)S(1)}, f32[1,332,268]{1,2,0:T(8,128)}, f32[1,332,268]{1,2,0:T(8,128)}) fusion(f32[1,332,268]{1,2,0:T(8,128)} %get-tuple-element.71, f32[1,332,268]{1,2,0:T(8,128)} %get-tuple-element.70, f32[1,332,268]{1,2,0:T(8,128)} %get-tuple-element.69, f32[1,332,268]{1,2,0:T(8,128)} %get-tuple-element.68, ...), kind=kLoop, calls=%fused_computation.82 | loop fusion | flops 1779520 | bytes 4271448 | tf_op jit(solution)/shard_map/sub | solution.py:137
  82.5 2.0 add.294
  84.5 2.0 divide_add_fusion
  86.5 1.9 gather_fusion.2
  88.4 1.9 gather_fusion.1
  90.3 2.7 %multiply_subtract_fusion = f32[1,332,268]{1,2,0:T(8,128)S(1)} fusion(f32[1,332,268]{1,2,0:T(8,128)} %get-tuple-element.71, f32[1,332,268]{1,2,0:T(8,128)} %get-tuple-element.70, f32[1,332,268]{1,2,0:T(8,128)} %get-tuple-element.69, f32[1,332,268]{1,2,0:T(8,128)} %get-tuple-element.68, f32[8,332,268]{1,2,0:T(8,128)S(1)} %pad_maximum_fusion, ...), kind=kLoop, calls=%fused_computation.74 | loop fusion | flops 1690544 | bytes 3559640 | tf_op jit(solution)/shard_map/sub | solution.py:137
  94.4 2.0 add.305
  96.4 2.2 add_bitcast_fusion.3
  98.6 1.9 gather_fusion
  100.5 9.1 %scatter_fusion = f32[332,268]{0,1:T(8,128)} fusion(f32[332,268]{0,1:T(8,128)} %get-tuple-element.84, s32[64]{0:T(128)S(1)} %get-tuple-element.110, f32[64]{0:T(128)S(1)} %get-tuple-element.108), kind=kCustom, calls=%fused_computation.3 | custom fusion | flops 64 | bytes 1280 | tf_op jit(solution)/shard_map/scatter-add | solution.py:146
  109.6 2.6 %multiply_bitcast_fusion.2 = (f32[332,268]{0,1:T(8,128)}, f32[1,332,268]{1,2,0:T(8,128)S(1)}, f32[1,332,268]{1,2,0:T(8,128)S(1)}) fusion(f32[1,332,268]{1,2,0:T(8,128)} %divide_add_fusion, f32[1,332,268]{1,2,0:T(8,128)} %get-tuple-element.66, f32[8,332,268]{1,2,0:T(8,128)S(1)} %pad_maximum_fusion, pred[268]{0:T(512)(128)(4,1)S(1)} %fusion.39, ...), kind=kLoop, calls=%fused_computation.67 | loop fusion | flops 1067712 | bytes 3915544 | tf_op jit(solution)/shard_map/reduce_sum | solution.py:168
  113.5 9.2 %scatter_fusion.1 = f32[332,268]{0,1:T(8,128)} fusion(f32[332,268]{0,1:T(8,128)} %fusion.23, s32[64]{0:T(128)S(1)} %get-tuple-element.110, f32[64]{0:T(128)S(1)} %get-tuple-element.107), kind=kCustom, calls=%fused_computation.4 | custom fusion | flops 64 | bytes 1280 | tf_op jit(solution)/shard_map/scatter-add | solution.py:146
  122.7 2.4 %multiply_bitcast_fusion.1 = (f32[332,268]{0,1:T(8,128)}, f32[1,332,268]{1,2,0:T(8,128)S(1)}, f32[1,332,268]{1,2,0:T(8,128)S(1)}) fusion(f32[1,332,268]{1,2,0:T(8,128)} %get-tuple-element.65, f32[8,332,268]{1,2,0:T(8,128)S(1)} %pad_maximum_fusion, pred[268]{0:T(512)(128)(4,1)S(1)} %fusion.39, pred[332]{0:T(512)(128)(4,1)S(1)} %fusion.38, ...), kind=kLoop, calls=%fused_computation.66 | loop fusion | flops 800784 | bytes 3559640 | tf_op jit(solution)/shard_map/reduce_sum | solution.py:168
  126.3 9.1 %scatter_fusion.2 = f32[332,268]{0,1:T(8,128)} fusion(f32[332,268]{0,1:T(8,128)} %fusion.21, s32[64]{0:T(128)S(1)} %get-tuple-element.110, f32[64]{0:T(128)S(1)} %get-tuple-element.62), kind=kCustom, calls=%fused_computation.5 | custom fusion | flops 64 | bytes 1280 | tf_op jit(solution)/shard_map/scatter-add | solution.py:146
  135.4 2.6 %multiply_bitcast_fusion = (f32[332,268]{0,1:T(8,128)S(1)}, f32[1,332,268]{1,2,0:T(8,128)}, f32[1,332,268]{1,2,0:T(8,128)}, f32[1,332,268]{1,2,0:T(8,128)S(1)}) fusion(f32[8,332,268]{1,2,0:T(8,128)S(1)} %pad_maximum_fusion, pred[268]{0:T(512)(128)(4,1)S(1)} %fusion.39, pred[332]{0:T(512)(128)(4,1)S(1)} %fusion.38, f32[1,332,268]{1,2,0:T(8,128)} %copy-done.26, ...), kind=kLoop, calls=%fused_computation.64 | loop fusion | flops 978736 | bytes 4627352 | tf_op jit(solution)/shard_map/reduce_sum | solution.py:168
  138.1 3.3 %fusion.32 = (f32[1,332,268]{1,2,0:T(8,128)S(1)}, f32[1,332,268]{1,2,0:T(8,128)S(1)}, f32[332,268]{0,1:T(8,128)S(1)}, f32[332,268]{0,1:T(8,128)S(1)}, f32[332,268]{0,1:T(8,128)S(1)}, /*index=5*/f32[1,332,268]{1,2,0:T(8,128)S(1)}) fusion(f32[1,332,268]{1,2,0:T(8,128)S(1)} %get-tuple-element.61, f32[1,332,268]{1,2,0:T(8,128)S(1)} %copy-done.32, ...), kind=kLoop, calls=%fused_computation.139 | loop fusion | flops 12723568 | bytes 4626752 | tf_op jit(solution)/shard_map/sub | solution.py:40
  143.2 17.1 %all-reduce.9.cloned.1.call-done = f32[2,320,256]{1,2,0:T(8,128)} async-done(((f32[2,320,256]{1,2,0:T(8,128)}), f32[2,320,256]{1,2,0:T(8,128)}) %all-reduce.9.cloned.1.call-update) | async-done | bytes 655376 | tf_op jit(solution)/shard_map/psum | solution.py:217
  161.5 3.7 %collective-permute-start.4 = (f32[2,1,256]{1,2,0:T(8,128)S(1)}, f32[2,1,256]{1,2,0:T(8,128)S(1)}, u32[]{:S(2)}, u32[]{:S(2)}) collective-permute-start(f32[2,1,256]{1,2,0:T(8,128)S(1)} %get-tuple-element.97), channel_id=1, source_target_pairs={{0,2},{2,4},{4,6},{1,3},{3,5},{5,7},{8,10},{10,12},{12,14},{9,11},... | collective-permute-start | bytes 6152 | tf_op jit(solution)/shard_map/ppermute | solution.py:18
  165.3 1.6 collective-permute-start.5
  166.8 4.3 %collective-permute-done.4 = f32[2,1,256]{1,2,0:T(8,128)S(1)} collective-permute-done((f32[2,1,256]{1,2,0:T(8,128)S(1)}, f32[2,1,256]{1,2,0:T(8,128)S(1)}, u32[]{:S(2)}, u32[]{:S(2)}) %collective-permute-start.4) | collective-permute-done | bytes 2080 | tf_op jit(solution)/shard_map/ppermute | solution.py:18
  171.2 4.5 %collective-permute-done.5 = f32[2,1,256]{1,2,0:T(8,128)S(1)} collective-permute-done((f32[2,1,256]{1,2,0:T(8,128)S(1)}, f32[2,1,256]{1,2,0:T(8,128)S(1)}, u32[]{:S(2)}, u32[]{:S(2)}) %collective-permute-start.5) | collective-permute-done | bytes 2080 | tf_op jit(solution)/shard_map/ppermute | solution.py:20
  176.5 3.4 %collective-permute-start.6 = (f32[2,322,1]{1,2,0:T(1,128)S(1)}, f32[2,322,1]{1,2,0:T(1,128)S(1)}, u32[]{:S(2)}, u32[]{:S(2)}) collective-permute-start(f32[2,322,1]{1,2,0:T(1,128)S(1)} %get-tuple-element.91), channel_id=1, source_target_pairs={{0,1},{2,3},{4,5},{6,7},{8,9},{10,11},{12,13},{14,15},{16,17},{18,... | collective-permute-start | bytes 7736 | tf_op jit(solution)/shard_map/ppermute | solution.py:18
  181.2 4.2 %collective-permute-done.7 = f32[2,322,1]{1,2,0:T(1,128)S(1)} collective-permute-done((f32[2,322,1]{1,2,0:T(1,128)S(1)}, f32[2,322,1]{1,2,0:T(1,128)S(1)}, u32[]{:S(2)}, u32[]{:S(2)}) %collective-permute-start.7) | collective-permute-done | bytes 2608 | tf_op jit(solution)/shard_map/ppermute | solution.py:20
  185.3 3.5 %fusion.9 = f32[2,320,256]{1,2,0:T(8,128)S(1)} fusion(f32[2,320,256]{1,2,0:T(8,128)} %all-reduce.9.cloned.1.call-done, f32[2,322,1]{1,2,0:T(1,128)S(1)} %collective-permute-done.7, f32[2,1,256]{1,2,0:T(8,128)S(1)} %collective-permute-done.5, f32[2,1,256]{1,2,0:T(8,128)S(1)} %collective-permute-done.4, f32[2,322,1]{1,2,0:T(1,128)S(1)} %collective-permute-done.6), kind=kLoop, calls=%fused_computation.29 | loop fusion | flops 2457600 | bytes 1319968 | tf_op jit(solution)/shard_map/add | solution.py:61
  189.0 3.4 %collective-permute-start.8 = (f32[2,1,256]{1,2,0:T(8,128)S(1)}, f32[2,1,256]{1,2,0:T(8,128)S(1)}, u32[]{:S(2)}, u32[]{:S(2)}) collective-permute-start(f32[2,1,256]{1,2,0:T(8,128)S(1)} %get-tuple-element.95), channel_id=1, source_target_pairs={{0,2},{2,4},{4,6},{1,3},{3,5},{5,7},{8,10},{10,12},{12,14},{9,11},... | collective-permute-start | bytes 6152 | tf_op jit(solution)/shard_map/ppermute | solution.py:18
  193.7 2.5 %collective-permute-done.8 = f32[2,1,256]{1,2,0:T(8,128)S(1)} collective-permute-done((f32[2,1,256]{1,2,0:T(8,128)S(1)}, f32[2,1,256]{1,2,0:T(8,128)S(1)}, u32[]{:S(2)}, u32[]{:S(2)}) %collective-permute-start.8) | collective-permute-done | bytes 2080 | tf_op jit(solution)/shard_map/ppermute | solution.py:18
  196.2 4.4 %collective-permute-done.9 = f32[2,1,256]{1,2,0:T(8,128)S(1)} collective-permute-done((f32[2,1,256]{1,2,0:T(8,128)S(1)}, f32[2,1,256]{1,2,0:T(8,128)S(1)}, u32[]{:S(2)}, u32[]{:S(2)}) %collective-permute-start.9) | collective-permute-done | bytes 2080 | tf_op jit(solution)/shard_map/ppermute | solution.py:20
  200.7 1.7 collective-permute-start.10
  203.8 1.5 slice_subtract_fusion.12
  207.9 1.9 fusion.3
  (151 shorter events, 32.6 us)
Async XLA Ops:
  7.2 11.5 %copy-start.44 = (f32[1,320,256]{2,1,0:T(8,128)S(1)}, f32[1,320,256]{2,1,0:T(8,128)}, u32[]{:S(2)}) copy-start(f32[1,320,256]{2,1,0:T(8,128)} %param.32) | copy-start | bytes 983044
  7.2 12.4 %copy-start.45 = (f32[1,320,256]{2,1,0:T(8,128)S(1)}, f32[1,320,256]{2,1,0:T(8,128)}, u32[]{:S(2)}) copy-start(f32[1,320,256]{2,1,0:T(8,128)} %param.33) | copy-start | bytes 983044
  7.2 153.2 %all-reduce.9.cloned.1.call-start = ((), (), s32[]{:S(2)}) async-start(), calls=%async_computation | async-start | bytes 1572864 | tf_op jit(solution)/shard_map/psum | solution.py:217
  19.8 14.1 %copy-start.42 = (f32[1,320,256]{1,2,0:T(8,128)S(1)}, f32[1,320,256]{1,2,0:T(8,128)}, u32[]{:S(2)}) copy-start(f32[1,320,256]{1,2,0:T(8,128)} %copy.82) | copy-start | bytes 983044
  19.8 14.1 %copy-start.41 = (f32[1,320,256]{1,2,0:T(8,128)S(1)}, f32[1,320,256]{1,2,0:T(8,128)}, u32[]{:S(2)}) copy-start(f32[1,320,256]{1,2,0:T(8,128)} %copy.83) | copy-start | bytes 983044
  19.8 14.2 %copy-start.40 = (f32[1,320,256]{1,2,0:T(8,128)S(1)}, f32[1,320,256]{1,2,0:T(8,128)}, u32[]{:S(2)}) copy-start(f32[1,320,256]{1,2,0:T(8,128)} %copy.84) | copy-start | bytes 983044
  34.1 21.4 %copy-start = (f32[8,320,256]{1,2,0:T(8,128)}, f32[8,320,256]{1,2,0:T(8,128)S(1)}, u32[]{:S(2)}) copy-start(f32[8,320,256]{1,2,0:T(8,128)S(1)} %constant_dynamic-update-slice_fusion) | copy-start | bytes 7864324
  34.1 13.2 %copy-start.46 = (f32[1,3,1]{1,2,0:T(1,128)S(1)}, f32[1,3,1]{1,2,0:T(1,128)}, u32[]{:S(2)}) copy-start(f32[1,3,1]{1,2,0:T(1,128)} %param.26) | copy-start | bytes 40
  34.1 13.9 %copy-start.47 = (s32[64]{0:T(128)S(1)}, s32[64]{0:T(128)}, u32[]{:S(2)}) copy-start(s32[64]{0:T(128)} %param.27) | copy-start | bytes 772
  34.1 13.9 %copy-start.48 = (s32[64]{0:T(128)S(1)}, s32[64]{0:T(128)}, u32[]{:S(2)}) copy-start(s32[64]{0:T(128)} %param.28) | copy-start | bytes 772
  34.1 13.9 %copy-start.50 = (s32[3]{0:T(128)S(1)}, s32[3]{0:T(128)}, u32[]{:S(2)}) copy-start(s32[3]{0:T(128)} %constant.129.clone.1) | copy-start | bytes 40
  37.6 16.6 %collective-permute-start.1 = (f32[8,6,256]{2,0,1:T(8,128)S(1)}, f32[8,6,256]{2,0,1:T(8,128)S(1)}, u32[]{:S(2)}, u32[]{:S(2)}) collective-permute-start(f32[8,6,256]{2,0,1:T(8,128)S(1)} %copy.87), channel_id=1, source_target_pairs={{2,0},{4,2},{6,4},{3,1},{5,3},{7,5},{10,8},{12,10},{14,12},{11,9},... | collective-permute-start | bytes 147464 | tf_op jit(solution)/shard_map/ppermute | solution.py:20
  40.4 12.4 %collective-permute-start = (f32[8,6,256]{2,0,1:T(8,128)S(1)}, f32[8,6,256]{2,0,1:T(8,128)S(1)}, u32[]{:S(2)}, u32[]{:S(2)}) collective-permute-start(f32[8,6,256]{2,0,1:T(8,128)S(1)} %copy.86), channel_id=1, source_target_pairs={{0,2},{2,4},{4,6},{1,3},{3,5},{5,7},{8,10},{10,12},{12,14},{9,11},... | collective-permute-start | bytes 147464 | tf_op jit(solution)/shard_map/ppermute | solution.py:18
  55.5 11.5 %copy-start.16 = (f32[8,6,256]{1,2,0:T(8,128)S(1)}, f32[8,6,256]{1,2,0:T(8,128)}, u32[]{:S(2)}) copy-start(f32[8,6,256]{1,2,0:T(8,128)} %copy.88) | copy-start | bytes 147460
  55.5 11.5 %copy-start.17 = (f32[8,6,256]{1,2,0:T(8,128)S(1)}, f32[8,6,256]{1,2,0:T(8,128)}, u32[]{:S(2)}) copy-start(f32[8,6,256]{1,2,0:T(8,128)} %copy.89) | copy-start | bytes 147460
  56.6 6.0 %collective-permute-start.2 = (f32[8,332,6]{1,2,0:T(8,128)S(1)}, f32[8,332,6]{1,2,0:T(8,128)S(1)}, u32[]{:S(2)}, u32[]{:S(2)}) collective-permute-start(f32[8,332,6]{1,2,0:T(8,128)S(1)} %get-tuple-element.81), channel_id=1, source_target_pairs={{0,1},{2,3},{4,5},{6,7},{8,9},{10,11},{12,13},{14,15},{16,17},{18,... | collective-permute-start | bytes 191240 | tf_op jit(solution)/shard_map/ppermute | solution.py:18
  60.4 6.5 %collective-permute-start.3 = (f32[8,332,6]{1,2,0:T(8,128)S(1)}, f32[8,332,6]{1,2,0:T(8,128)S(1)}, u32[]{:S(2)}, u32[]{:S(2)}) collective-permute-start(f32[8,332,6]{1,2,0:T(8,128)S(1)} %get-tuple-element.82), channel_id=1, source_target_pairs={{1,0},{3,2},{5,4},{7,6},{9,8},{11,10},{13,12},{15,14},{17,16},{19,... | collective-permute-start | bytes 191240 | tf_op jit(solution)/shard_map/ppermute | solution.py:20
  70.2 2.7 %copy-start.31 = (f32[1,332,268]{1,2,0:T(8,128)}, f32[1,332,268]{1,2,0:T(8,128)S(1)}, u32[]{:S(2)}) copy-start(f32[1,332,268]{1,2,0:T(8,128)S(1)} %get-tuple-element.86) | copy-start | bytes 1067716
  90.3 10.2 %copy-start.49 = (f32[1,3,64]{2,0,1:T(1,128)S(1)}, f32[1,3,64]{2,0,1:T(1,128)}, u32[]{:S(2)}) copy-start(f32[1,3,64]{2,0,1:T(1,128)} %param.29) | copy-start | bytes 2308
  109.6 2.6 %copy-start.8 = (f32[1,332,268]{1,2,0:T(8,128)S(1)}, f32[1,332,268]{1,2,0:T(8,128)}, u32[]{:S(2)}) copy-start(f32[1,332,268]{1,2,0:T(8,128)} %get-tuple-element.70) | copy-start | bytes 1067716
  109.6 2.6 %copy-start.11 = (f32[1,332,268]{1,2,0:T(8,128)S(1)}, f32[1,332,268]{1,2,0:T(8,128)}, u32[]{:S(2)}) copy-start(f32[1,332,268]{1,2,0:T(8,128)} %get-tuple-element.71) | copy-start | bytes 1067716
  109.6 2.6 %copy-start.18 = (f32[332,268]{0,1:T(8,128)S(1)}, f32[332,268]{0,1:T(8,128)}, u32[]{:S(2)}) copy-start(f32[332,268]{0,1:T(8,128)} %scatter_fusion) | copy-start | bytes 1067716
  135.4 2.6 %copy-start.1 = (f32[1,332,268]{1,2,0:T(8,128)S(1)}, f32[1,332,268]{1,2,0:T(8,128)}, u32[]{:S(2)}) copy-start(f32[1,332,268]{1,2,0:T(8,128)} %divide_add_fusion) | copy-start | bytes 1067716
  135.4 2.6 %copy-start.15 = (f32[1,332,268]{1,2,0:T(8,128)S(1)}, f32[1,332,268]{1,2,0:T(8,128)}, u32[]{:S(2)}) copy-start(f32[1,332,268]{1,2,0:T(8,128)} %copy-done.14) | copy-start | bytes 1067716
  135.4 2.6 %copy-start.23 = (f32[332,268]{0,1:T(8,128)S(1)}, f32[332,268]{0,1:T(8,128)}, u32[]{:S(2)}) copy-start(f32[332,268]{0,1:T(8,128)} %copy-done.22) | copy-start | bytes 1067716
  135.4 2.7 %copy-start.28 = (f32[1,332,268]{1,2,0:T(8,128)S(1)}, f32[1,332,268]{1,2,0:T(8,128)}, u32[]{:S(2)}) copy-start(f32[1,332,268]{1,2,0:T(8,128)} %copy-done.27) | copy-start | bytes 1067716
  135.4 2.7 %copy-start.30 = (f32[1,332,268]{1,2,0:T(8,128)S(1)}, f32[1,332,268]{1,2,0:T(8,128)}, u32[]{:S(2)}) copy-start(f32[1,332,268]{1,2,0:T(8,128)} %copy-done.29) | copy-start | bytes 1067716
  135.4 2.7 %copy-start.32 = (f32[1,332,268]{1,2,0:T(8,128)S(1)}, f32[1,332,268]{1,2,0:T(8,128)}, u32[]{:S(2)}) copy-start(f32[1,332,268]{1,2,0:T(8,128)} %copy-done.31) | copy-start | bytes 1067716
  138.0 4.3 %copy-start.24 = (f32[1,332,268]{1,2,0:T(8,128)}, f32[1,332,268]{1,2,0:T(8,128)S(1)}, u32[]{:S(2)}) copy-start(f32[1,332,268]{1,2,0:T(8,128)S(1)} %get-tuple-element.61) | copy-start | bytes 1067716
  138.0 3.4 %copy-start.36 = (f32[332,268]{0,1:T(8,128)S(1)}, f32[332,268]{0,1:T(8,128)}, u32[]{:S(2)}) copy-start(f32[332,268]{0,1:T(8,128)} %get-tuple-element.52) | copy-start | bytes 1067716
  138.0 3.4 %copy-start.37 = (f32[332,268]{0,1:T(8,128)S(1)}, f32[332,268]{0,1:T(8,128)}, u32[]{:S(2)}) copy-start(f32[332,268]{0,1:T(8,128)} %get-tuple-element.55) | copy-start | bytes 1067716
  143.2 50.5 %copy-start.25 = (f32[1,332,268]{1,2,0:T(8,128)S(1)}, f32[1,332,268]{1,2,0:T(8,128)}, u32[]{:S(2)}) copy-start(f32[1,332,268]{1,2,0:T(8,128)} %copy-done.24) | copy-start | bytes 1067716
  161.5 9.7 %collective-permute-start.4 = (f32[2,1,256]{1,2,0:T(8,128)S(1)}, f32[2,1,256]{1,2,0:T(8,128)S(1)}, u32[]{:S(2)}, u32[]{:S(2)}) collective-permute-start(f32[2,1,256]{1,2,0:T(8,128)S(1)} %get-tuple-element.97), channel_id=1, source_target_pairs={{0,2},{2,4},{4,6},{1,3},{3,5},{5,7},{8,10},{10,12},{12,14},{9,11},... | collective-permute-start | bytes 6152 | tf_op jit(solution)/shard_map/ppermute | solution.py:18
  165.2 38.5 %copy-start.4 = (f32[1,332,268]{1,2,0:T(8,128)S(1)}, f32[1,332,268]{1,2,0:T(8,128)}, u32[]{:S(2)}) copy-start(f32[1,332,268]{1,2,0:T(8,128)} %get-tuple-element.68) | copy-start | bytes 1067716
  165.2 38.5 %copy-start.7 = (f32[1,332,268]{1,2,0:T(8,128)S(1)}, f32[1,332,268]{1,2,0:T(8,128)}, u32[]{:S(2)}) copy-start(f32[1,332,268]{1,2,0:T(8,128)} %get-tuple-element.69) | copy-start | bytes 1067716
  165.2 38.5 %copy-start.10 = (f32[1,332,268]{1,2,0:T(8,128)S(1)}, f32[1,332,268]{1,2,0:T(8,128)}, u32[]{:S(2)}) copy-start(f32[1,332,268]{1,2,0:T(8,128)} %get-tuple-element.70) | copy-start | bytes 1067716
  165.2 38.5 %copy-start.13 = (f32[1,332,268]{1,2,0:T(8,128)S(1)}, f32[1,332,268]{1,2,0:T(8,128)}, u32[]{:S(2)}) copy-start(f32[1,332,268]{1,2,0:T(8,128)} %get-tuple-element.71) | copy-start | bytes 1067716
  165.3 38.5 %copy-start.20 = (f32[332,268]{0,1:T(8,128)S(1)}, f32[332,268]{0,1:T(8,128)}, u32[]{:S(2)}) copy-start(f32[332,268]{0,1:T(8,128)} %scatter_fusion.2) | copy-start | bytes 1067716
  165.3 38.5 %copy-start.38 = (f32[1,332,268]{1,2,0:T(8,128)S(1)}, f32[1,332,268]{1,2,0:T(8,128)}, u32[]{:S(2)}) copy-start(f32[1,332,268]{1,2,0:T(8,128)} %get-tuple-element.59) | copy-start | bytes 1067716
  165.3 38.5 %copy-start.39 = (f32[1,332,268]{1,2,0:T(8,128)S(1)}, f32[1,332,268]{1,2,0:T(8,128)}, u32[]{:S(2)}) copy-start(f32[1,332,268]{1,2,0:T(8,128)} %get-tuple-element.60) | copy-start | bytes 1067716
  165.3 10.3 %collective-permute-start.5 = (f32[2,1,256]{1,2,0:T(8,128)S(1)}, f32[2,1,256]{1,2,0:T(8,128)S(1)}, u32[]{:S(2)}, u32[]{:S(2)}) collective-permute-start(f32[2,1,256]{1,2,0:T(8,128)S(1)} %get-tuple-element.98), channel_id=1, source_target_pairs={{2,0},{4,2},{6,4},{3,1},{5,3},{7,5},{10,8},{12,10},{14,12},{11,9},... | collective-permute-start | bytes 6152 | tf_op jit(solution)/shard_map/ppermute | solution.py:20
  176.5 4.7 %collective-permute-start.6 = (f32[2,322,1]{1,2,0:T(1,128)S(1)}, f32[2,322,1]{1,2,0:T(1,128)S(1)}, u32[]{:S(2)}, u32[]{:S(2)}) collective-permute-start(f32[2,322,1]{1,2,0:T(1,128)S(1)} %get-tuple-element.91), channel_id=1, source_target_pairs={{0,1},{2,3},{4,5},{6,7},{8,9},{10,11},{12,13},{14,15},{16,17},{18,... | collective-permute-start | bytes 7736 | tf_op jit(solution)/shard_map/ppermute | solution.py:18
  179.9 5.5 %collective-permute-start.7 = (f32[2,322,1]{1,2,0:T(1,128)S(1)}, f32[2,322,1]{1,2,0:T(1,128)S(1)}, u32[]{:S(2)}, u32[]{:S(2)}) collective-permute-start(f32[2,322,1]{1,2,0:T(1,128)S(1)} %get-tuple-element.92), channel_id=1, source_target_pairs={{1,0},{3,2},{5,4},{7,6},{9,8},{11,10},{13,12},{15,14},{17,16},{19,... | collective-permute-start | bytes 7736 | tf_op jit(solution)/shard_map/ppermute | solution.py:20
  189.0 7.3 %collective-permute-start.8 = (f32[2,1,256]{1,2,0:T(8,128)S(1)}, f32[2,1,256]{1,2,0:T(8,128)S(1)}, u32[]{:S(2)}, u32[]{:S(2)}) collective-permute-start(f32[2,1,256]{1,2,0:T(8,128)S(1)} %get-tuple-element.95), channel_id=1, source_target_pairs={{0,2},{2,4},{4,6},{1,3},{3,5},{5,7},{8,10},{10,12},{12,14},{9,11},... | collective-permute-start | bytes 6152 | tf_op jit(solution)/shard_map/ppermute | solution.py:18
  192.4 8.3 %collective-permute-start.9 = (f32[2,1,256]{1,2,0:T(8,128)S(1)}, f32[2,1,256]{1,2,0:T(8,128)S(1)}, u32[]{:S(2)}, u32[]{:S(2)}) collective-permute-start(f32[2,1,256]{1,2,0:T(8,128)S(1)} %get-tuple-element.96), channel_id=1, source_target_pairs={{2,0},{4,2},{6,4},{3,1},{5,3},{7,5},{10,8},{12,10},{14,12},{11,9},... | collective-permute-start | bytes 6152 | tf_op jit(solution)/shard_map/ppermute | solution.py:20
  200.6 3.1 %copy-start.43 = (f32[2,1,256]{1,2,0:T(8,128)}, f32[2,1,256]{1,2,0:T(8,128)S(1)}, u32[]{:S(2)}) copy-start(f32[2,1,256]{1,2,0:T(8,128)S(1)} %collective-permute-done.9) | copy-start | bytes 6148
  200.7 6.3 %collective-permute-start.10 = (f32[2,322,1]{1,2,0:T(1,128)S(1)}, f32[2,322,1]{1,2,0:T(1,128)S(1)}, u32[]{:S(2)}, u32[]{:S(2)}) collective-permute-start(f32[2,322,1]{1,2,0:T(1,128)S(1)} %get-tuple-element.89), channel_id=1, source_target_pairs={{0,1},{2,3},{4,5},{6,7},{8,9},{10,11},{12,13},{14,15},{16,17},{18,... | collective-permute-start | bytes 7736 | tf_op jit(solution)/shard_map/ppermute | solution.py:18
  202.4 5.5 %collective-permute-start.11 = (f32[2,322,1]{1,2,0:T(1,128)S(1)}, f32[2,322,1]{1,2,0:T(1,128)S(1)}, u32[]{:S(2)}, u32[]{:S(2)}) collective-permute-start(f32[2,322,1]{1,2,0:T(1,128)S(1)} %get-tuple-element.90), channel_id=1, source_target_pairs={{1,0},{3,2},{5,4},{7,6},{9,8},{11,10},{13,12},{15,14},{17,16},{19,... | collective-permute-start | bytes 7736 | tf_op jit(solution)/shard_map/ppermute | solution.py:20
  (16 other events, 26.1 us)
Sparse Core Ops, SparseCore 0:
  143.4 16.9 all-reduce.8
where the time goes:
time: 220 us; the launch traced here: 218 us
  other arithmetic  81.3 us (37%)
  local copies, waits for them, and re-layouts  43.8 us (20%)
  waiting for transfers between devices  43 us (20%)
  starting transfers between devices  29.6 us (13%)
  between operations  20.8 us (9%)
    scatter-add x3, other arithmetic, inject(): return adjoint_field.at[:, obs_lx, obs_ly].add(mismatch)  27.4 us
    ppermute x6, starting transfers between devices, padded_2(): lax.ppermute(tail, axis, [(i, (i + 1) % count) for i in range(ends)])  21.5 us
    unnamed x118, local copies, waits for them, and re-layouts  20.3 us
    ppermute x6, waiting for transfers between devices, padded_2(): lax.ppermute(head, axis, [((i + 1) % count, i) for i in range(ends)])  18.2 us
    psum x1, waiting for transfers between devices, on_device(): summed = lax.psum(stacked, 'test')  17.1 us
    unnamed x2, other arithmetic  11.8 us
    ppermute x6, starting transfers between devices, padded_2(): lax.ppermute(head, axis, [((i + 1) % count, i) for i in range(ends)])  8.02 us
    ppermute x6, waiting for transfers between devices, padded_2(): lax.ppermute(tail, axis, [(i, (i + 1) % count) for i in range(ends)])  7.71 us
  transfers between devices with their start and end apart: 13, of which 9 were waited for; matrix products, arithmetic and copies ran while one was open for 4% of the time, Pallas kernels for 0%

commit v1 on v0

--- a/solution.py
+++ b/solution.py
@@ -214,7 +214,7 @@
         matrix_end,
     )
     stacked = jnp.stack([grad_cond, grad_shape], 0)
-    summed = lax.psum(stacked, "test")
+    summed = jnp.sum(lax.all_gather(stacked, "test"), axis=0)
     smoothed = smooth(summed)
     return (smoothed[0], smoothed[1], fracture_adj, matrix_adj)
 

time: 220 us -> 209 us (0.950)
  waiting for transfers between devices: 43 us -> 32.5 us
  other arithmetic: 81.3 us -> 78.2 us
  local copies, waits for them, and re-layouts: 43.8 us -> 46.2 us
    psum x1 -> x0, waiting for transfers between devices: 17.1 us -> none  [on_device(): summed = lax.psum(stacked, 'test')]
    all_gather x0 -> x1, waiting for transfers between devices: none -> 7.38 us  [on_device(): summed = jnp.sum(lax.all_gather(stacked, 'test'), axis=0)]
    add x2, other arithmetic: 5.42 us -> 1.67 us  [smooth(): grad_field + blend_rate * (nearby[0] + nearby[1] + nearby[2] + nearby[3]...]
    unnamed x118 -> x117, local copies, waits for them, and re-layouts: 20.3 us -> 22.6 us
  transfers between devices with their start and end apart: 13 -> 13, of which waited for: 9 -> 8; matrix products, arithmetic and copies ran while one was open for 4% -> 5% of each run, Pallas kernels for 0% -> 0%
where the time goes in v1:
time: 209 us; the launch traced here: 207 us
  other arithmetic  78.2 us (37%)
  local copies, waits for them, and re-layouts  46.2 us (22%)
  waiting for transfers between devices  32.5 us (16%)
  starting transfers between devices  29.8 us (14%)
  between operations  20.4 us (10%)
    scatter-add x3, other arithmetic, inject(): return adjoint_field.at[:, obs_lx, obs_ly].add(mismatch)  27.3 us
    unnamed x117, local copies, waits for them, and re-layouts  22.6 us
    ppermute x6, starting transfers between devices, padded_2(): lax.ppermute(tail, axis, [(i, (i + 1) % count) for i in range(ends)])  21.5 us
    ppermute x6, waiting for transfers between devices, padded_2(): lax.ppermute(head, axis, [((i + 1) % count, i) for i in range(ends)])  17.4 us
    unnamed x2, other arithmetic  11.9 us
    ppermute x6, starting transfers between devices, padded_2(): lax.ppermute(head, axis, [((i + 1) % count, i) for i in range(ends)])  8.24 us
    ppermute x6, waiting for transfers between devices, padded_2(): lax.ppermute(tail, axis, [(i, (i + 1) % count) for i in range(ends)])  7.74 us
    reduce_sum x3, other arithmetic, margin_window(): jnp.sum(swap_rate * (fracture - matrix), axis=0)  7.54 us
  transfers between devices with their start and end apart: 13, of which 8 were waited for; matrix products, arithmetic and copies ran while one was open for 5% of the time, Pallas kernels for 0%

profile of v1, /device:TPU:0, one launch (start us, length us, event | category | flops | bytes accessed | tf_op | source)
XLA Modules:
  0.0 207.1 jit_solution(12476625196430995167)
XLA Ops:
  7.2 2.0 fusion.52
  9.2 1.9 copy.68
  11.1 1.9 copy.69
  13.0 1.9 copy.70
  14.9 1.9 copy.78
  16.8 1.9 copy.79
  22.0 6.5 %bitcast_dynamic-update-slice_fusion.1 = (f32[8,320,256]{1,2,0:T(8,128)S(1)}, pred[320,256]{0,1:T(8,128)(4,1)S(1)}, pred[320,256]{0,1:T(8,128)(4,1)S(1)}, pred[3...) fusion(f32[8,320,256]{1,2,0:T(8,128)S(1)} %bitcast_dynamic-upda, ...), kind=kLoop, calls=%fused_computation.121 | loop fusion | flops 1310720 | bytes 1507360
  28.5 5.4 %bitcast_dynamic-update-slice_fusion = f32[8,320,256]{1,2,0:T(8,128)S(1)} fusion(f32[8,320,256]{1,2,0:T(8,128)S(1)} %get-tuple-element.72, pred[320,256]{0,1:T(8,128)(4,1)S(1)} %get-tuple-element.80, pred[320,256]{0,1:T(8,128)(4,1)S(1)} %get-tuple-element.79, pred[320,256]{0,1:T(8,128)(4,1)S(1)} %get-tuple-element.78, ...), kind=kLoop, calls=%fused_computation.120 | loop fusion | flops 655360 | bytes 1179680
  34.2 1.9 fusion.49
  36.1 1.5 copy.83
  38.9 1.6 copy.82
  40.5 5.6 %collective-permute-start = (f32[8,6,256]{2,0,1:T(8,128)S(1)}, f32[8,6,256]{2,0,1:T(8,128)S(1)}, u32[]{:S(2)}, u32[]{:S(2)}) collective-permute-start(f32[8,6,256]{2,0,1:T(8,128)S(1)} %copy.82), channel_id=1, source_target_pairs={{0,2},{2,4},{4,6},{1,3},{3,5},{5,7},{8,10},{10,12},{12,14},{9,11},... | collective-permute-start | bytes 147464 | tf_op jit(solution)/shard_map/ppermute | solution.py:18
  56.2 3.8 %collective-permute-start.2 = (f32[8,332,6]{1,2,0:T(8,128)S(1)}, f32[8,332,6]{1,2,0:T(8,128)S(1)}, u32[]{:S(2)}, u32[]{:S(2)}) collective-permute-start(f32[8,332,6]{1,2,0:T(8,128)S(1)} %get-tuple-element.81), channel_id=1, source_target_pairs={{0,1},{2,3},{4,5},{6,7},{8,9},{10,11},{12,13},{14,15},{16,17},{18,... | collective-permute-start | bytes 191240 | tf_op jit(solution)/shard_map/ppermute | solution.py:18
  62.3 4.3 %collective-permute-done.3 = f32[8,332,6]{1,2,0:T(8,128)S(1)} collective-permute-done((f32[8,332,6]{1,2,0:T(8,128)S(1)}, f32[8,332,6]{1,2,0:T(8,128)S(1)}, u32[]{:S(2)}, u32[]{:S(2)}) %collective-permute-start.3) | collective-permute-done | bytes 63776 | tf_op jit(solution)/shard_map/ppermute | solution.py:20
  66.6 3.2 %pad_maximum_fusion = f32[8,332,268]{1,2,0:T(8,128)S(1)} fusion(f32[8,332,6]{1,2,0:T(8,128)S(1)} %collective-permute-done.3, f32[8,6,256]{1,2,0:T(8,128)S(1)} %copy-done.17, f32[8,320,256]{1,2,0:T(8,128)} %copy-done, f32[8,6,256]{1,2,0:T(8,128)S(1)} %copy-done.16, f32[8,332,6]{1,2,0:T(8,128)S(1)} %collective-permute-done.2), kind=kLoop, calls=%fused_computation.6 | loop fusion | flops 2847232 | bytes 5694464 | tf_op jit(solution)/shard_map/concatenate | solution.py:16
  70.6 1.9 add_subtract_fusion.2
  77.9 2.8 %add_subtract_fusion.1 = (f32[1,332,268]{1,2,0:T(8,128)S(1)}, f32[1,332,268]{1,2,0:T(8,128)}, f32[1,332,268]{1,2,0:T(8,128)}) fusion(f32[1,332,268]{1,2,0:T(8,128)} %get-tuple-element.71, f32[1,332,268]{1,2,0:T(8,128)} %get-tuple-element.70, f32[1,332,268]{1,2,0:T(8,128)} %get-tuple-element.69, f32[1,332,268]{1,2,0:T(8,128)} %get-tuple-element.68, ...), kind=kLoop, calls=%fused_computation.82 | loop fusion | flops 1779520 | bytes 4271448 | tf_op jit(solution)/shard_map/sub | solution.py:137
  82.0 2.0 add.292
  84.0 2.0 divide_add_fusion
  86.0 1.9 gather_fusion.2
  87.9 1.9 gather_fusion.1
  89.8 2.8 %multiply_subtract_fusion = f32[1,332,268]{1,2,0:T(8,128)S(1)} fusion(f32[1,332,268]{1,2,0:T(8,128)} %get-tuple-element.71, f32[1,332,268]{1,2,0:T(8,128)} %get-tuple-element.70, f32[1,332,268]{1,2,0:T(8,128)} %get-tuple-element.69, f32[1,332,268]{1,2,0:T(8,128)} %get-tuple-element.68, f32[8,332,268]{1,2,0:T(8,128)S(1)} %pad_maximum_fusion, ...), kind=kLoop, calls=%fused_computation.74 | loop fusion | flops 1690544 | bytes 3559640 | tf_op jit(solution)/shard_map/sub | solution.py:137
  94.0 2.1 %add.303 = f32[1,332,268]{1,2,0:T(8,128)} dynamic-update-slice(f32[1,332,268]{1,2,0:T(8,128)} %copy-done.33, f32[1,1,1]{1,2,0:T(1,128)} %fusion.55, s32[]{:T(128)} %constant.116.clone.1, s32[]{:T(128)} %bitcast.27, s32[]{:T(128)} %bitcast.29) | dynamic-update-slice | bytes 12 | tf_op jit(solution)/shard_map/add | solution.py:137
  96.1 2.2 %add_bitcast_fusion.3 = (f32[332,268]{0,1:T(8,128)}, f32[332,268]{0,1:T(8,128)}) fusion(f32[1,332,268]{1,2,0:T(8,128)} %divide_add_fusion, f32[1,332,268]{1,2,0:T(8,128)} %add.303, f32[8,332,268]{1,2,0:T(8,128)S(1)} %pad_maximum_fusion, pred[268]{0:T(512)(128)(4,1)S(1)} %fusion.39, pred[332]{0:T(512)(128)(4,1)S(1)} %fusion.38), kind=kLoop, calls=%fused_computation.73 | loop fusion | flops 355904 | bytes 2136024 | tf_op jit(solution)/shard_map/add | solution.py:136
  98.3 1.9 gather_fusion
  100.2 9.1 %scatter_fusion = f32[332,268]{0,1:T(8,128)} fusion(f32[332,268]{0,1:T(8,128)} %get-tuple-element.84, s32[64]{0:T(128)S(1)} %get-tuple-element.110, f32[64]{0:T(128)S(1)} %get-tuple-element.108), kind=kCustom, calls=%fused_computation.3 | custom fusion | flops 64 | bytes 1280 | tf_op jit(solution)/shard_map/scatter-add | solution.py:146
  109.3 2.6 %multiply_bitcast_fusion.2 = (f32[332,268]{0,1:T(8,128)}, f32[1,332,268]{1,2,0:T(8,128)S(1)}, f32[1,332,268]{1,2,0:T(8,128)S(1)}) fusion(f32[1,332,268]{1,2,0:T(8,128)} %divide_add_fusion, f32[1,332,268]{1,2,0:T(8,128)} %get-tuple-element.66, f32[8,332,268]{1,2,0:T(8,128)S(1)} %pad_maximum_fusion, pred[268]{0:T(512)(128)(4,1)S(1)} %fusion.39, ...), kind=kLoop, calls=%fused_computation.67 | loop fusion | flops 1067712 | bytes 3915544 | tf_op jit(solution)/shard_map/reduce_sum | solution.py:168
  113.1 9.1 %scatter_fusion.1 = f32[332,268]{0,1:T(8,128)} fusion(f32[332,268]{0,1:T(8,128)} %fusion.23, s32[64]{0:T(128)S(1)} %get-tuple-element.110, f32[64]{0:T(128)S(1)} %get-tuple-element.107), kind=kCustom, calls=%fused_computation.4 | custom fusion | flops 64 | bytes 1280 | tf_op jit(solution)/shard_map/scatter-add | solution.py:146
  122.2 2.4 %multiply_bitcast_fusion.1 = (f32[332,268]{0,1:T(8,128)}, f32[1,332,268]{1,2,0:T(8,128)S(1)}, f32[1,332,268]{1,2,0:T(8,128)S(1)}) fusion(f32[1,332,268]{1,2,0:T(8,128)} %get-tuple-element.65, f32[8,332,268]{1,2,0:T(8,128)S(1)} %pad_maximum_fusion, pred[268]{0:T(512)(128)(4,1)S(1)} %fusion.39, pred[332]{0:T(512)(128)(4,1)S(1)} %fusion.38, ...), kind=kLoop, calls=%fused_computation.66 | loop fusion | flops 800784 | bytes 3559640 | tf_op jit(solution)/shard_map/reduce_sum | solution.py:168
  125.8 9.1 %scatter_fusion.2 = f32[332,268]{0,1:T(8,128)} fusion(f32[332,268]{0,1:T(8,128)} %fusion.21, s32[64]{0:T(128)S(1)} %get-tuple-element.110, f32[64]{0:T(128)S(1)} %get-tuple-element.62), kind=kCustom, calls=%fused_computation.5 | custom fusion | flops 64 | bytes 1280 | tf_op jit(solution)/shard_map/scatter-add | solution.py:146
  134.9 2.6 %multiply_bitcast_fusion = (f32[332,268]{0,1:T(8,128)S(1)}, f32[1,332,268]{1,2,0:T(8,128)}, f32[1,332,268]{1,2,0:T(8,128)}, f32[1,332,268]{1,2,0:T(8,128)S(1)}) fusion(f32[8,332,268]{1,2,0:T(8,128)S(1)} %pad_maximum_fusion, pred[268]{0:T(512)(128)(4,1)S(1)} %fusion.39, pred[332]{0:T(512)(128)(4,1)S(1)} %fusion.38, f32[1,332,268]{1,2,0:T(8,128)} %copy-done.26, ...), kind=kLoop, calls=%fused_computation.64 | loop fusion | flops 978736 | bytes 4627352 | tf_op jit(solution)/shard_map/reduce_sum | solution.py:168
  137.6 3.3 %fusion.32 = (f32[1,332,268]{1,2,0:T(8,128)S(1)}, f32[1,332,268]{1,2,0:T(8,128)S(1)}, f32[332,268]{0,1:T(8,128)S(1)}, f32[332,268]{0,1:T(8,128)S(1)}, f32[332,268]{0,1:T(8,128)S(1)}, /*index=5*/f32[1,332,268]{1,2,0:T(8,128)S(1)}) fusion(f32[1,332,268]{1,2,0:T(8,128)S(1)} %get-tuple-element.61, f32[1,332,268]{1,2,0:T(8,128)S(1)} %copy-done.32, ...), kind=kLoop, calls=%fused_computation.139 | loop fusion | flops 12723568 | bytes 4626752 | tf_op jit(solution)/shard_map/sub | solution.py:40
  143.0 7.4 %all-gather.3.cloned.1.call-done = f32[4,320,256]{2,1,0:T(8,128)} async-done(((f32[2,320,256]{2,1,0:T(8,128)}), f32[4,320,256]{2,1,0:T(8,128)}) %all-gather.3.cloned.1.call-update) | async-done | bytes 1310736 | tf_op jit(solution)/shard_map/all_gather | solution.py:217
  150.4 1.5 reduce_sum.41
  152.3 3.7 %collective-permute-start.4 = (f32[2,1,256]{1,2,0:T(8,128)S(1)}, f32[2,1,256]{1,2,0:T(8,128)S(1)}, u32[]{:S(2)}, u32[]{:S(2)}) collective-permute-start(f32[2,1,256]{1,2,0:T(8,128)S(1)} %get-tuple-element.97), channel_id=1, source_target_pairs={{0,2},{2,4},{4,6},{1,3},{3,5},{5,7},{8,10},{10,12},{12,14},{9,11},... | collective-permute-start | bytes 6152 | tf_op jit(solution)/shard_map/ppermute | solution.py:18
  156.0 1.6 collective-permute-start.5
  157.6 4.4 %collective-permute-done.4 = f32[2,1,256]{1,2,0:T(8,128)S(1)} collective-permute-done((f32[2,1,256]{1,2,0:T(8,128)S(1)}, f32[2,1,256]{1,2,0:T(8,128)S(1)}, u32[]{:S(2)}, u32[]{:S(2)}) %collective-permute-start.4) | collective-permute-done | bytes 2080 | tf_op jit(solution)/shard_map/ppermute | solution.py:18
  162.0 4.5 %collective-permute-done.5 = f32[2,1,256]{1,2,0:T(8,128)S(1)} collective-permute-done((f32[2,1,256]{1,2,0:T(8,128)S(1)}, f32[2,1,256]{1,2,0:T(8,128)S(1)}, u32[]{:S(2)}, u32[]{:S(2)}) %collective-permute-start.5) | collective-permute-done | bytes 2080 | tf_op jit(solution)/shard_map/ppermute | solution.py:20
  166.5 3.4 %collective-permute-start.6 = (f32[2,322,1]{1,2,0:T(1,128)S(1)}, f32[2,322,1]{1,2,0:T(1,128)S(1)}, u32[]{:S(2)}, u32[]{:S(2)}) collective-permute-start(f32[2,322,1]{1,2,0:T(1,128)S(1)} %get-tuple-element.91), channel_id=1, source_target_pairs={{0,1},{2,3},{4,5},{6,7},{8,9},{10,11},{12,13},{14,15},{16,17},{18,... | collective-permute-start | bytes 7736 | tf_op jit(solution)/shard_map/ppermute | solution.py:18
  171.2 4.2 %collective-permute-done.7 = f32[2,322,1]{1,2,0:T(1,128)S(1)} collective-permute-done((f32[2,322,1]{1,2,0:T(1,128)S(1)}, f32[2,322,1]{1,2,0:T(1,128)S(1)}, u32[]{:S(2)}, u32[]{:S(2)}) %collective-permute-start.7) | collective-permute-done | bytes 2608 | tf_op jit(solution)/shard_map/ppermute | solution.py:20
  176.4 3.4 %collective-permute-start.8 = (f32[2,1,256]{1,2,0:T(8,128)S(1)}, f32[2,1,256]{1,2,0:T(8,128)S(1)}, u32[]{:S(2)}, u32[]{:S(2)}) collective-permute-start(f32[2,1,256]{1,2,0:T(8,128)S(1)} %get-tuple-element.95), channel_id=1, source_target_pairs={{0,2},{2,4},{4,6},{1,3},{3,5},{5,7},{8,10},{10,12},{12,14},{9,11},... | collective-permute-start | bytes 6152 | tf_op jit(solution)/shard_map/ppermute | solution.py:18
  181.1 2.5 %collective-permute-done.8 = f32[2,1,256]{1,2,0:T(8,128)S(1)} collective-permute-done((f32[2,1,256]{1,2,0:T(8,128)S(1)}, f32[2,1,256]{1,2,0:T(8,128)S(1)}, u32[]{:S(2)}, u32[]{:S(2)}) %collective-permute-start.8) | collective-permute-done | bytes 2080 | tf_op jit(solution)/shard_map/ppermute | solution.py:18
  183.6 4.4 %collective-permute-done.9 = f32[2,1,256]{1,2,0:T(8,128)S(1)} collective-permute-done((f32[2,1,256]{1,2,0:T(8,128)S(1)}, f32[2,1,256]{1,2,0:T(8,128)S(1)}, u32[]{:S(2)}, u32[]{:S(2)}) %collective-permute-start.9) | collective-permute-done | bytes 2080 | tf_op jit(solution)/shard_map/ppermute | solution.py:20
  188.1 1.7 collective-permute-start.10
  189.8 1.5 collective-permute-start.11
  191.4 2.4 %slice_subtract_fusion.12 = (f32[1,320,256]{1,2,0:T(8,128)}, f32[1,320,256]{1,2,0:T(8,128)}) fusion(f32[1,332,268]{1,2,0:T(8,128)S(1)} %copy-done.39, f32[1,332,268]{1,2,0:T(8,128)S(1)} %copy-done.38, f32[1,332,268]{1,2,0:T(8,128)S(1)} %get-tuple-element.102, f32[1,332,268]{1,2,0:T(8,128)S(1)} %copy-done.13, f32[1,332,268]{1,2,0:T(8,128)S(1)} %copy-done.25, ...), kind=kLoop, calls=%fused_computation.97 | loop fusion | flops 983040 | bytes 4587520 | tf_op jit(solution)/shard_map/sub | solution.py:170
  193.8 1.9 copy.100
  195.7 1.9 copy.99
  (152 shorter events, 31.7 us)
Async XLA Ops:
  7.2 11.5 %copy-start.43 = (f32[1,320,256]{2,1,0:T(8,128)S(1)}, f32[1,320,256]{2,1,0:T(8,128)}, u32[]{:S(2)}) copy-start(f32[1,320,256]{2,1,0:T(8,128)} %param.32) | copy-start | bytes 983044
  7.2 12.4 %copy-start.44 = (f32[1,320,256]{2,1,0:T(8,128)S(1)}, f32[1,320,256]{2,1,0:T(8,128)}, u32[]{:S(2)}) copy-start(f32[1,320,256]{2,1,0:T(8,128)} %param.33) | copy-start | bytes 983044
  7.2 143.2 %all-gather.3.cloned.1.call-start = ((), (), s32[]{:S(2)}) async-start(), calls=%async_computation | async-start | bytes 1966080 | tf_op jit(solution)/shard_map/all_gather | solution.py:217
  19.8 14.2 %copy-start.42 = (f32[1,320,256]{1,2,0:T(8,128)S(1)}, f32[1,320,256]{1,2,0:T(8,128)}, u32[]{:S(2)}) copy-start(f32[1,320,256]{1,2,0:T(8,128)} %copy.78) | copy-start | bytes 983044
  19.8 14.2 %copy-start.41 = (f32[1,320,256]{1,2,0:T(8,128)S(1)}, f32[1,320,256]{1,2,0:T(8,128)}, u32[]{:S(2)}) copy-start(f32[1,320,256]{1,2,0:T(8,128)} %copy.79) | copy-start | bytes 983044
  19.8 14.2 %copy-start.40 = (f32[1,320,256]{1,2,0:T(8,128)S(1)}, f32[1,320,256]{1,2,0:T(8,128)}, u32[]{:S(2)}) copy-start(f32[1,320,256]{1,2,0:T(8,128)} %copy.80) | copy-start | bytes 983044
  34.1 21.0 %copy-start = (f32[8,320,256]{1,2,0:T(8,128)}, f32[8,320,256]{1,2,0:T(8,128)S(1)}, u32[]{:S(2)}) copy-start(f32[8,320,256]{1,2,0:T(8,128)S(1)} %constant_dynamic-update-slice_fusion) | copy-start | bytes 7864324
  34.1 13.3 %copy-start.45 = (f32[1,3,1]{1,2,0:T(1,128)S(1)}, f32[1,3,1]{1,2,0:T(1,128)}, u32[]{:S(2)}) copy-start(f32[1,3,1]{1,2,0:T(1,128)} %param.26) | copy-start | bytes 40
  34.1 13.9 %copy-start.46 = (s32[64]{0:T(128)S(1)}, s32[64]{0:T(128)}, u32[]{:S(2)}) copy-start(s32[64]{0:T(128)} %param.27) | copy-start | bytes 772
  34.1 13.9 %copy-start.47 = (s32[64]{0:T(128)S(1)}, s32[64]{0:T(128)}, u32[]{:S(2)}) copy-start(s32[64]{0:T(128)} %param.28) | copy-start | bytes 772
  34.2 13.9 %copy-start.49 = (s32[3]{0:T(128)S(1)}, s32[3]{0:T(128)}, u32[]{:S(2)}) copy-start(s32[3]{0:T(128)} %constant.129.clone.1) | copy-start | bytes 40
  37.6 16.2 %collective-permute-start.1 = (f32[8,6,256]{2,0,1:T(8,128)S(1)}, f32[8,6,256]{2,0,1:T(8,128)S(1)}, u32[]{:S(2)}, u32[]{:S(2)}) collective-permute-start(f32[8,6,256]{2,0,1:T(8,128)S(1)} %copy.83), channel_id=1, source_target_pairs={{2,0},{4,2},{6,4},{3,1},{5,3},{7,5},{10,8},{12,10},{14,12},{11,9},... | collective-permute-start | bytes 147464 | tf_op jit(solution)/shard_map/ppermute | solution.py:20
  40.5 12.0 %collective-permute-start = (f32[8,6,256]{2,0,1:T(8,128)S(1)}, f32[8,6,256]{2,0,1:T(8,128)S(1)}, u32[]{:S(2)}, u32[]{:S(2)}) collective-permute-start(f32[8,6,256]{2,0,1:T(8,128)S(1)} %copy.82), channel_id=1, source_target_pairs={{0,2},{2,4},{4,6},{1,3},{3,5},{5,7},{8,10},{10,12},{12,14},{9,11},... | collective-permute-start | bytes 147464 | tf_op jit(solution)/shard_map/ppermute | solution.py:18
  55.1 11.5 %copy-start.16 = (f32[8,6,256]{1,2,0:T(8,128)S(1)}, f32[8,6,256]{1,2,0:T(8,128)}, u32[]{:S(2)}) copy-start(f32[8,6,256]{1,2,0:T(8,128)} %copy.84) | copy-start | bytes 147460
  55.1 11.5 %copy-start.17 = (f32[8,6,256]{1,2,0:T(8,128)S(1)}, f32[8,6,256]{1,2,0:T(8,128)}, u32[]{:S(2)}) copy-start(f32[8,6,256]{1,2,0:T(8,128)} %copy.85) | copy-start | bytes 147460
  56.2 6.0 %collective-permute-start.2 = (f32[8,332,6]{1,2,0:T(8,128)S(1)}, f32[8,332,6]{1,2,0:T(8,128)S(1)}, u32[]{:S(2)}, u32[]{:S(2)}) collective-permute-start(f32[8,332,6]{1,2,0:T(8,128)S(1)} %get-tuple-element.81), channel_id=1, source_target_pairs={{0,1},{2,3},{4,5},{6,7},{8,9},{10,11},{12,13},{14,15},{16,17},{18,... | collective-permute-start | bytes 191240 | tf_op jit(solution)/shard_map/ppermute | solution.py:18
  60.1 6.5 %collective-permute-start.3 = (f32[8,332,6]{1,2,0:T(8,128)S(1)}, f32[8,332,6]{1,2,0:T(8,128)S(1)}, u32[]{:S(2)}, u32[]{:S(2)}) collective-permute-start(f32[8,332,6]{1,2,0:T(8,128)S(1)} %get-tuple-element.82), channel_id=1, source_target_pairs={{1,0},{3,2},{5,4},{7,6},{9,8},{11,10},{13,12},{15,14},{17,16},{19,... | collective-permute-start | bytes 191240 | tf_op jit(solution)/shard_map/ppermute | solution.py:20
  69.9 2.7 %copy-start.31 = (f32[1,332,268]{1,2,0:T(8,128)}, f32[1,332,268]{1,2,0:T(8,128)S(1)}, u32[]{:S(2)}) copy-start(f32[1,332,268]{1,2,0:T(8,128)S(1)} %get-tuple-element.86) | copy-start | bytes 1067716
  89.8 10.4 %copy-start.48 = (f32[1,3,64]{2,0,1:T(1,128)S(1)}, f32[1,3,64]{2,0,1:T(1,128)}, u32[]{:S(2)}) copy-start(f32[1,3,64]{2,0,1:T(1,128)} %param.29) | copy-start | bytes 2308
  109.3 2.6 %copy-start.5 = (f32[1,332,268]{1,2,0:T(8,128)S(1)}, f32[1,332,268]{1,2,0:T(8,128)}, u32[]{:S(2)}) copy-start(f32[1,332,268]{1,2,0:T(8,128)} %get-tuple-element.69) | copy-start | bytes 1067716
  109.3 2.6 %copy-start.8 = (f32[1,332,268]{1,2,0:T(8,128)S(1)}, f32[1,332,268]{1,2,0:T(8,128)}, u32[]{:S(2)}) copy-start(f32[1,332,268]{1,2,0:T(8,128)} %get-tuple-element.70) | copy-start | bytes 1067716
  109.3 2.6 %copy-start.11 = (f32[1,332,268]{1,2,0:T(8,128)S(1)}, f32[1,332,268]{1,2,0:T(8,128)}, u32[]{:S(2)}) copy-start(f32[1,332,268]{1,2,0:T(8,128)} %get-tuple-element.71) | copy-start | bytes 1067716
  109.3 2.6 %copy-start.18 = (f32[332,268]{0,1:T(8,128)S(1)}, f32[332,268]{0,1:T(8,128)}, u32[]{:S(2)}) copy-start(f32[332,268]{0,1:T(8,128)} %scatter_fusion) | copy-start | bytes 1067716
  134.9 2.6 %copy-start.1 = (f32[1,332,268]{1,2,0:T(8,128)S(1)}, f32[1,332,268]{1,2,0:T(8,128)}, u32[]{:S(2)}) copy-start(f32[1,332,268]{1,2,0:T(8,128)} %divide_add_fusion) | copy-start | bytes 1067716
  134.9 2.6 %copy-start.15 = (f32[1,332,268]{1,2,0:T(8,128)S(1)}, f32[1,332,268]{1,2,0:T(8,128)}, u32[]{:S(2)}) copy-start(f32[1,332,268]{1,2,0:T(8,128)} %copy-done.14) | copy-start | bytes 1067716
  134.9 2.6 %copy-start.23 = (f32[332,268]{0,1:T(8,128)S(1)}, f32[332,268]{0,1:T(8,128)}, u32[]{:S(2)}) copy-start(f32[332,268]{0,1:T(8,128)} %copy-done.22) | copy-start | bytes 1067716
  134.9 2.6 %copy-start.28 = (f32[1,332,268]{1,2,0:T(8,128)S(1)}, f32[1,332,268]{1,2,0:T(8,128)}, u32[]{:S(2)}) copy-start(f32[1,332,268]{1,2,0:T(8,128)} %copy-done.27) | copy-start | bytes 1067716
  134.9 2.6 %copy-start.30 = (f32[1,332,268]{1,2,0:T(8,128)S(1)}, f32[1,332,268]{1,2,0:T(8,128)}, u32[]{:S(2)}) copy-start(f32[1,332,268]{1,2,0:T(8,128)} %copy-done.29) | copy-start | bytes 1067716
  134.9 2.6 %copy-start.32 = (f32[1,332,268]{1,2,0:T(8,128)S(1)}, f32[1,332,268]{1,2,0:T(8,128)}, u32[]{:S(2)}) copy-start(f32[1,332,268]{1,2,0:T(8,128)} %copy-done.31) | copy-start | bytes 1067716
  137.5 4.3 %copy-start.24 = (f32[1,332,268]{1,2,0:T(8,128)}, f32[1,332,268]{1,2,0:T(8,128)S(1)}, u32[]{:S(2)}) copy-start(f32[1,332,268]{1,2,0:T(8,128)S(1)} %get-tuple-element.61) | copy-start | bytes 1067716
  137.5 3.4 %copy-start.36 = (f32[332,268]{0,1:T(8,128)S(1)}, f32[332,268]{0,1:T(8,128)}, u32[]{:S(2)}) copy-start(f32[332,268]{0,1:T(8,128)} %get-tuple-element.52) | copy-start | bytes 1067716
  137.5 3.4 %copy-start.37 = (f32[332,268]{0,1:T(8,128)S(1)}, f32[332,268]{0,1:T(8,128)}, u32[]{:S(2)}) copy-start(f32[332,268]{0,1:T(8,128)} %get-tuple-element.55) | copy-start | bytes 1067716
  151.9 29.2 %copy-start.25 = (f32[1,332,268]{1,2,0:T(8,128)S(1)}, f32[1,332,268]{1,2,0:T(8,128)}, u32[]{:S(2)}) copy-start(f32[1,332,268]{1,2,0:T(8,128)} %copy-done.24) | copy-start | bytes 1067716
  152.3 9.7 %collective-permute-start.4 = (f32[2,1,256]{1,2,0:T(8,128)S(1)}, f32[2,1,256]{1,2,0:T(8,128)S(1)}, u32[]{:S(2)}, u32[]{:S(2)}) collective-permute-start(f32[2,1,256]{1,2,0:T(8,128)S(1)} %get-tuple-element.97), channel_id=1, source_target_pairs={{0,2},{2,4},{4,6},{1,3},{3,5},{5,7},{8,10},{10,12},{12,14},{9,11},... | collective-permute-start | bytes 6152 | tf_op jit(solution)/shard_map/ppermute | solution.py:18
  156.0 35.3 %copy-start.4 = (f32[1,332,268]{1,2,0:T(8,128)S(1)}, f32[1,332,268]{1,2,0:T(8,128)}, u32[]{:S(2)}) copy-start(f32[1,332,268]{1,2,0:T(8,128)} %get-tuple-element.68) | copy-start | bytes 1067716
  156.0 35.3 %copy-start.7 = (f32[1,332,268]{1,2,0:T(8,128)S(1)}, f32[1,332,268]{1,2,0:T(8,128)}, u32[]{:S(2)}) copy-start(f32[1,332,268]{1,2,0:T(8,128)} %get-tuple-element.69) | copy-start | bytes 1067716
  156.0 35.3 %copy-start.10 = (f32[1,332,268]{1,2,0:T(8,128)S(1)}, f32[1,332,268]{1,2,0:T(8,128)}, u32[]{:S(2)}) copy-start(f32[1,332,268]{1,2,0:T(8,128)} %get-tuple-element.70) | copy-start | bytes 1067716
  156.0 35.3 %copy-start.13 = (f32[1,332,268]{1,2,0:T(8,128)S(1)}, f32[1,332,268]{1,2,0:T(8,128)}, u32[]{:S(2)}) copy-start(f32[1,332,268]{1,2,0:T(8,128)} %get-tuple-element.71) | copy-start | bytes 1067716
  156.0 35.3 %copy-start.20 = (f32[332,268]{0,1:T(8,128)S(1)}, f32[332,268]{0,1:T(8,128)}, u32[]{:S(2)}) copy-start(f32[332,268]{0,1:T(8,128)} %scatter_fusion.2) | copy-start | bytes 1067716
  156.0 35.3 %copy-start.38 = (f32[1,332,268]{1,2,0:T(8,128)S(1)}, f32[1,332,268]{1,2,0:T(8,128)}, u32[]{:S(2)}) copy-start(f32[1,332,268]{1,2,0:T(8,128)} %get-tuple-element.59) | copy-start | bytes 1067716
  156.0 35.3 %copy-start.39 = (f32[1,332,268]{1,2,0:T(8,128)S(1)}, f32[1,332,268]{1,2,0:T(8,128)}, u32[]{:S(2)}) copy-start(f32[1,332,268]{1,2,0:T(8,128)} %get-tuple-element.60) | copy-start | bytes 1067716
  156.0 10.4 %collective-permute-start.5 = (f32[2,1,256]{1,2,0:T(8,128)S(1)}, f32[2,1,256]{1,2,0:T(8,128)S(1)}, u32[]{:S(2)}, u32[]{:S(2)}) collective-permute-start(f32[2,1,256]{1,2,0:T(8,128)S(1)} %get-tuple-element.98), channel_id=1, source_target_pairs={{2,0},{4,2},{6,4},{3,1},{5,3},{7,5},{10,8},{12,10},{14,12},{11,9},... | collective-permute-start | bytes 6152 | tf_op jit(solution)/shard_map/ppermute | solution.py:20
  166.5 4.7 %collective-permute-start.6 = (f32[2,322,1]{1,2,0:T(1,128)S(1)}, f32[2,322,1]{1,2,0:T(1,128)S(1)}, u32[]{:S(2)}, u32[]{:S(2)}) collective-permute-start(f32[2,322,1]{1,2,0:T(1,128)S(1)} %get-tuple-element.91), channel_id=1, source_target_pairs={{0,1},{2,3},{4,5},{6,7},{8,9},{10,11},{12,13},{14,15},{16,17},{18,... | collective-permute-start | bytes 7736 | tf_op jit(solution)/shard_map/ppermute | solution.py:18
  169.9 5.5 %collective-permute-start.7 = (f32[2,322,1]{1,2,0:T(1,128)S(1)}, f32[2,322,1]{1,2,0:T(1,128)S(1)}, u32[]{:S(2)}, u32[]{:S(2)}) collective-permute-start(f32[2,322,1]{1,2,0:T(1,128)S(1)} %get-tuple-element.92), channel_id=1, source_target_pairs={{1,0},{3,2},{5,4},{7,6},{9,8},{11,10},{13,12},{15,14},{17,16},{19,... | collective-permute-start | bytes 7736 | tf_op jit(solution)/shard_map/ppermute | solution.py:20
  176.4 7.3 %collective-permute-start.8 = (f32[2,1,256]{1,2,0:T(8,128)S(1)}, f32[2,1,256]{1,2,0:T(8,128)S(1)}, u32[]{:S(2)}, u32[]{:S(2)}) collective-permute-start(f32[2,1,256]{1,2,0:T(8,128)S(1)} %get-tuple-element.95), channel_id=1, source_target_pairs={{0,2},{2,4},{4,6},{1,3},{3,5},{5,7},{8,10},{10,12},{12,14},{9,11},... | collective-permute-start | bytes 6152 | tf_op jit(solution)/shard_map/ppermute | solution.py:18
  179.8 8.3 %collective-permute-start.9 = (f32[2,1,256]{1,2,0:T(8,128)S(1)}, f32[2,1,256]{1,2,0:T(8,128)S(1)}, u32[]{:S(2)}, u32[]{:S(2)}) collective-permute-start(f32[2,1,256]{1,2,0:T(8,128)S(1)} %get-tuple-element.96), channel_id=1, source_target_pairs={{2,0},{4,2},{6,4},{3,1},{5,3},{7,5},{10,8},{12,10},{14,12},{11,9},... | collective-permute-start | bytes 6152 | tf_op jit(solution)/shard_map/ppermute | solution.py:20
  188.1 9.4 %collective-permute-start.10 = (f32[2,322,1]{1,2,0:T(1,128)S(1)}, f32[2,322,1]{1,2,0:T(1,128)S(1)}, u32[]{:S(2)}, u32[]{:S(2)}) collective-permute-start(f32[2,322,1]{1,2,0:T(1,128)S(1)} %get-tuple-element.89), channel_id=1, source_target_pairs={{0,1},{2,3},{4,5},{6,7},{8,9},{10,11},{12,13},{14,15},{16,17},{18,... | collective-permute-start | bytes 7736 | tf_op jit(solution)/shard_map/ppermute | solution.py:18
  189.8 7.8 %collective-permute-start.11 = (f32[2,322,1]{1,2,0:T(1,128)S(1)}, f32[2,322,1]{1,2,0:T(1,128)S(1)}, u32[]{:S(2)}, u32[]{:S(2)}) collective-permute-start(f32[2,322,1]{1,2,0:T(1,128)S(1)} %get-tuple-element.90), channel_id=1, source_target_pairs={{1,0},{3,2},{5,4},{7,6},{9,8},{11,10},{13,12},{15,14},{17,16},{19,... | collective-permute-start | bytes 7736 | tf_op jit(solution)/shard_map/ppermute | solution.py:20
  (15 other events, 23.4 us)
Sparse Core Ops, SparseCore 0:
  143.1 7.2 all-gather.2
